TPU v7x, 512 devices: a whole 4x4x16 slice. The times are simulated.
512 devices in a mesh: grp: 8 (over x, core), own: 64 (over z, y).
Axes of the slice: x: 4, y: 4, z: 16, core: 2. Of those that a mesh axis runs over, the one named last changes fastest.
Arguments:
- left: bfloat16 [32768, 128, 64], P(('grp', 'own')), may hold values from -0.75 to 0.75
- right: bfloat16 [32768, 128, 64], P(('grp', 'own')), may hold values from -0.75 to 0.75
- values: bfloat16 [32768, 128], P(('grp', 'own')), may hold values from -6 to 6
- core: bfloat16 [10240, 64, 64], P(('grp', 'own')), may hold values from -6 to 6
- tile_slice: int32 [32768], P(('grp', 'own')), may hold values from 0 to 10239, as said below
- tile_fill: int32 [32768], P(('grp', 'own')), may hold values from 64 to 128
Outputs:
- new_core: bfloat16 [10240, 64, 64], P(('grp', 'own'))
- new_left: bfloat16 [32768, 128, 64], P(('grp', 'own'))
Inputs may be any that keep to these rules, and one draw needn't show every extreme that they name: `tile_slice`: call j // 20 the block of slice j and its remainder mod 64 its class. Among the tiles of one device at most 2 have slices of one class; in every group of 64 consecutive devices some class gets exactly 2 tiles from every device of the group.
All inputs are finite; a program needn't handle non-finite values.
Results may differ from a plain program's by a relative error of at most 0.0052.
Values may be sent and summed in bfloat16 or wider, within the bound.
No kernel may reach another device: no remote copies, remote signals or barrier semaphores. Data moves between devices by JAX's collectives and lax.ppermute only.
A program may use at most 64 MiB of HBM per device.

v0:
```python
import jax
import jax.numpy as jnp
from jax import lax
from jax.sharding import PartitionSpec as P


def tile_terms(left_tiles, right_tiles, value_tiles, fill_counts, slice_tables):
    tile_rows = left_tiles.shape[1]
    projected = jnp.einsum(
        "sea,sab->seb", left_tiles, slice_tables, preferred_element_type=jnp.float32
    )
    predicted = jnp.sum(projected * right_tiles.astype(jnp.float32), axis=-1)
    live_rows = jnp.arange(tile_rows)[None, :] < fill_counts[:, None]
    residual = jnp.where(live_rows, predicted - value_tiles.astype(jnp.float32), 0.0)
    weighted = (residual[:, :, None] * left_tiles.astype(jnp.float32)).astype(jnp.bfloat16)
    return jnp.einsum("sea,seb->sab", weighted, right_tiles, preferred_element_type=jnp.float32)


def body(left, right, values, core, tile_slice, tile_fill):
    owners = lax.axis_size("own")
    groups = lax.axis_size("grp")
    tile_count, tile_rows, rank_width = left.shape
    per_device = core.shape[0]
    local_count = groups * per_device
    slot_cap = 2 * tile_count // owners
    slot_total = owners * slot_cap
    dev_block = tile_slice // per_device
    target_owner = dev_block % owners
    local_slice = dev_block // owners * per_device + tile_slice % per_device
    positions = jnp.arange(tile_count)
    same_owner = target_owner[:, None] == target_owner[None, :]
    earlier = positions[None, :] < positions[:, None]
    rank_among = jnp.sum((same_owner & earlier).astype(jnp.int32), axis=1)
    slot_of_tile = target_owner * slot_cap + rank_among
    slot_match = slot_of_tile[None, :] == jnp.arange(slot_total)[:, None]
    slot_live = jnp.any(slot_match, axis=1)
    tile_of_slot = jnp.sum(jnp.where(slot_match, positions[None, :], 0), axis=1)
    send_slice = jnp.where(slot_live, local_slice[tile_of_slot], 0)
    old_tables = lax.all_gather(core, "grp", axis=0, tiled=True)
    send_left = left[tile_of_slot]
    send_right = right[tile_of_slot]
    send_values = values[tile_of_slot]
    send_fill = jnp.where(slot_live, tile_fill[tile_of_slot], 0)
    got_left, got_right, got_values, got_slice, got_fill = (
        lax.all_to_all(send_left, "own", split_axis=0, concat_axis=0, tiled=True),
        lax.all_to_all(send_right, "own", split_axis=0, concat_axis=0, tiled=True),
        lax.all_to_all(send_values, "own", split_axis=0, concat_axis=0, tiled=True),
        lax.all_to_all(send_slice, "own", split_axis=0, concat_axis=0, tiled=True),
        lax.all_to_all(send_fill, "own", split_axis=0, concat_axis=0, tiled=True),
    )
    tile_grad = tile_terms(got_left, got_right, got_values, got_fill, old_tables[got_slice])
    selector = (got_slice[:, None] == jnp.arange(local_count)[None, :]).astype(jnp.float32)
    grad_part = jnp.dot(
        selector.T,
        tile_grad.reshape(slot_total, rank_width * rank_width),
        precision=lax.Precision.HIGHEST,
        preferred_element_type=jnp.float32,
    ).reshape(local_count, rank_width, rank_width)
    grad_whole = lax.psum(grad_part, "grp")
    new_tables = (old_tables.astype(jnp.float32) - grad_whole).astype(jnp.bfloat16)
    new_mine = lax.dynamic_slice_in_dim(
        new_tables, lax.axis_index("grp") * per_device, per_device, 0
    )
    refreshed = jnp.einsum(
        "sea,sab->seb", got_left, new_tables[got_slice], preferred_element_type=jnp.float32
    ).astype(jnp.bfloat16)
    returned = lax.all_to_all(refreshed, "own", split_axis=0, concat_axis=0, tiled=True)
    new_left = returned[slot_of_tile]
    return (new_mine, new_left)


def solution(mesh):
    return jax.shard_map(
        body,
        mesh=mesh,
        in_specs=(
            P(("grp", "own"), None, None),
            P(("grp", "own"), None, None),
            P(("grp", "own"), None),
            P(("grp", "own"), None, None),
            P(("grp", "own")),
            P(("grp", "own")),
        ),
        out_specs=(P(("grp", "own"), None, None), P(("grp", "own"), None, None)),
        check_vma=False,
    )
```

profile of v0, /device:TPU:7, one launch (start us, length us, event | category | flops | bytes accessed | tf_op | source)
XLA Modules:
  0.0 528.3 jit_solution(8652673713095691326)
XLA Ops:
  9.6 1.6 gather_fusion.1
  12.0 18.5 %all-to-all-start.1 = ((s32[64,2,1]{1,2,0:T(1,128)}), s32[64,2,1]{1,2,0:T(1,128)S(1)}, u32[]{:S(2)}, u32[]{:S(2)}) async-start(s32[64,2,1]{1,2,0:T(1,128)} %bitcast.4), calls=%async_computation.1 | async-start | bytes 65536 | tf_op jit(solution)/shard_map/all_to_all | solution.py:49
  31.2 12.7 %all-to-all-done.1 = s32[64,2,1]{1,2,0:T(1,128)S(1)} async-done(((s32[64,2,1]{1,2,0:T(1,128)}), s32[64,2,1]{1,2,0:T(1,128)S(1)}, u32[]{:S(2)}, u32[]{:S(2)}) %all-to-all-start.1) | async-done | bytes 544 | tf_op jit(solution)/shard_map/all_to_all | solution.py:49
  43.8 4.6 all-to-all-start
  48.4 2.1 gather_fusion.4
  50.6 11.4 %all-to-all-done = s32[64,2,1]{1,2,0:T(1,128)S(1)} async-done(((s32[64,2,1]{1,2,0:T(1,128)}), s32[64,2,1]{1,2,0:T(1,128)S(1)}, u32[]{:S(2)}, u32[]{:S(2)}) %all-to-all-start) | async-done | bytes 544 | tf_op jit(solution)/shard_map/all_to_all | solution.py:48
  61.9 4.7 all-to-all-start.3
  66.6 3.4 gather_fusion.2
  70.0 90.1 %all-to-all-done.3 = bf16[128,128,64]{1,2,0:T(8,128)(2,1)S(1)} async-done(((bf16[128,128,64]{1,2,0:T(8,128)(2,1)}), bf16[128,128,64]{1,2,0:T(8,128)(2,1)S(1)}, u32[]{:S(2)}, u32[]{:S(2)}) %all-to-all-start.3) | async-done | bytes 2097184 | tf_op jit(solution)/shard_map/all_to_all | solution.py:46
  160.2 1.3 copy-done.1
  161.5 10.7 %all-to-all-start.2 = ((bf16[128,128,64]{1,2,0:T(8,128)(2,1)}), bf16[128,128,64]{1,2,0:T(8,128)(2,1)S(1)}, u32[]{:S(2)}, u32[]{:S(2)}) async-start(bf16[128,128,64]{1,2,0:T(8,128)(2,1)} %gather_fusion.2), calls=%async_computation.2 | async-start | bytes 4194304 | tf_op jit(solution)/shard_map/all_to_all | solution.py:45
  172.9 1.3 gather_fusion.5
  176.7 34.6 %all-gather.2.cloned.1.call-done = bf16[160,64,64]{2,1,0:T(8,128)(2,1)} async-done(((bf16[20,64,64]{2,1,0:T(8,128)(2,1)}), bf16[160,64,64]{2,1,0:T(8,128)(2,1)}) %all-gather.2.cloned.1.call-update) | async-done | bytes 1310736 | tf_op jit(solution)/shard_map/all_gather | solution.py:39
  211.3 3.9 gather_fusion.3
  215.2 50.7 %all-to-all-done.2 = bf16[128,128,64]{1,2,0:T(8,128)(2,1)S(1)} async-done(((bf16[128,128,64]{1,2,0:T(8,128)(2,1)}), bf16[128,128,64]{1,2,0:T(8,128)(2,1)S(1)}, u32[]{:S(2)}, u32[]{:S(2)}) %all-to-all-start.2) | async-done | bytes 2097184 | tf_op jit(solution)/shard_map/all_to_all | solution.py:45
  265.9 11.0 %all-to-all-start.4 = ((bf16[64,2,128]{2,1,0:T(2,128)(2,1)}), bf16[64,2,128]{2,1,0:T(2,128)(2,1)S(1)}, u32[]{:S(2)}, u32[]{:S(2)}) async-start(bf16[64,2,128]{2,1,0:T(2,128)(2,1)} %bitcast.6), calls=%async_computation.4 | async-start | bytes 65536 | tf_op jit(solution)/shard_map/all_to_all | solution.py:47
  277.1 3.2 multiply_reduce_fusion
  280.4 9.9 %all-to-all-done.4 = bf16[64,2,128]{2,1,0:T(2,128)(2,1)S(1)} async-done(((bf16[64,2,128]{2,1,0:T(2,128)(2,1)}), bf16[64,2,128]{2,1,0:T(2,128)(2,1)S(1)}, u32[]{:S(2)}, u32[]{:S(2)}) %all-to-all-start.4) | async-done | bytes 32800 | tf_op jit(solution)/shard_map/all_to_all | solution.py:47
  290.4 4.8 fusion
  295.2 4.8 copy.30
  299.9 5.4 %fusion.1 = f32[160,64,64]{0,2,1:T(8,128)} fusion(f32[128,64,64]{0,2,1:T(8,128)} %copy.30, s32[128]{0:T(128)S(1)} %eq.50), kind=kOutput, calls=%fused_computation.12 | convolution fusion | flops 1006653440 | bytes 4719104 | tf_op jit(solution)/shard_map/dot_general | solution.py:53
  305.3 4.9 copy.26
  310.3 75.1 %all-reduce.2.cloned.1.call-done = f32[160,64,64]{0,2,1:T(8,128)} async-done(((f32[160,64,64]{0,2,1:T(8,128)}), f32[160,64,64]{0,2,1:T(8,128)}) %all-reduce.2.cloned.1.call-update) | async-done | bytes 2621456 | tf_op jit(solution)/shard_map/psum | solution.py:59
  385.4 5.0 subtract_convert_fusion
  390.4 5.0 copy.31
  395.4 3.9 gather_fusion.6
  399.3 3.8 convolution_convert_fusion
  403.0 15.8 %all-to-all-start.5 = ((bf16[128,128,64]{1,2,0:T(8,128)(2,1)}), bf16[128,128,64]{1,2,0:T(8,128)(2,1)}, u32[]{:S(2)}, u32[]{:S(2)}) async-start(bf16[128,128,64]{1,2,0:T(8,128)(2,1)} %convolution_convert_fusion), calls=%async_computation.5 | async-start | bytes 4194304 | tf_op jit(solution)/shard_map/all_to_all | solution.py:67
  418.8 1.5 constant_dynamic-slice_fusion
  420.3 2.6 copy.33
  422.8 95.4 %all-to-all-done.5 = bf16[128,128,64]{1,2,0:T(8,128)(2,1)} async-done(((bf16[128,128,64]{1,2,0:T(8,128)(2,1)}), bf16[128,128,64]{1,2,0:T(8,128)(2,1)}, u32[]{:S(2)}, u32[]{:S(2)}) %all-to-all-start.5) | async-done | bytes 2097184 | tf_op jit(solution)/shard_map/all_to_all | solution.py:67
  518.3 3.2 gather_fusion.7
  (33 shorter events, 7.4 us)
Async XLA Ops:
  7.2 41.3 %copy-start = (bf16[64,128,64]{1,2,0:T(8,128)(2,1)S(1)}, bf16[64,128,64]{1,2,0:T(8,128)(2,1)}, u32[]{:S(2)}) copy-start(bf16[64,128,64]{1,2,0:T(8,128)(2,1)} %param.7) | copy-start | bytes 3145732
  12.0 31.9 %all-to-all-start.1 = ((s32[64,2,1]{1,2,0:T(1,128)}), s32[64,2,1]{1,2,0:T(1,128)S(1)}, u32[]{:S(2)}, u32[]{:S(2)}) async-start(s32[64,2,1]{1,2,0:T(1,128)} %bitcast.4), calls=%async_computation.1 | async-start | bytes 65536 | tf_op jit(solution)/shard_map/all_to_all | solution.py:49
  43.8 18.1 %all-to-all-start = ((s32[64,2,1]{1,2,0:T(1,128)}), s32[64,2,1]{1,2,0:T(1,128)S(1)}, u32[]{:S(2)}, u32[]{:S(2)}) async-start(s32[64,2,1]{1,2,0:T(1,128)} %bitcast.2), calls=%async_computation | async-start | bytes 65536 | tf_op jit(solution)/shard_map/all_to_all | solution.py:48
  61.9 98.2 %all-to-all-start.3 = ((bf16[128,128,64]{1,2,0:T(8,128)(2,1)}), bf16[128,128,64]{1,2,0:T(8,128)(2,1)S(1)}, u32[]{:S(2)}, u32[]{:S(2)}) async-start(bf16[128,128,64]{1,2,0:T(8,128)(2,1)} %gather_fusion.4), calls=%async_computation.3 | async-start | bytes 4194304 | tf_op jit(solution)/shard_map/all_to_all | solution.py:46
  70.0 102.9 %copy-start.3 = (bf16[64,128]{1,0:T(8,128)(2,1)S(1)}, bf16[64,128]{1,0:T(8,128)(2,1)}, u32[]{:S(2)}) copy-start(bf16[64,128]{1,0:T(8,128)(2,1)} %param.8) | copy-start | bytes 49156
  160.2 1.3 copy-start.1
  161.5 104.4 %all-to-all-start.2 = ((bf16[128,128,64]{1,2,0:T(8,128)(2,1)}), bf16[128,128,64]{1,2,0:T(8,128)(2,1)S(1)}, u32[]{:S(2)}, u32[]{:S(2)}) async-start(bf16[128,128,64]{1,2,0:T(8,128)(2,1)} %gather_fusion.2), calls=%async_computation.2 | async-start | bytes 4194304 | tf_op jit(solution)/shard_map/all_to_all | solution.py:45
  172.2 39.1 %all-gather.2.cloned.1.call-start = ((), (), s32[]{:S(2)}) async-start(), calls=%async_computation.6 | async-start | bytes 2949120 | tf_op jit(solution)/shard_map/all_gather | solution.py:39
  265.9 24.4 %all-to-all-start.4 = ((bf16[64,2,128]{2,1,0:T(2,128)(2,1)}), bf16[64,2,128]{2,1,0:T(2,128)(2,1)S(1)}, u32[]{:S(2)}, u32[]{:S(2)}) async-start(bf16[64,2,128]{2,1,0:T(2,128)(2,1)} %bitcast.6), calls=%async_computation.4 | async-start | bytes 65536 | tf_op jit(solution)/shard_map/all_to_all | solution.py:47
  276.9 108.5 %all-reduce.2.cloned.1.call-start = ((), (), s32[]{:S(2)}) async-start(), calls=%async_computation.7 | async-start | bytes 8388608 | tf_op jit(solution)/shard_map/psum | solution.py:59
  403.0 15.8 %copy-start.2 = (bf16[160,64,64]{0,2,1:T(8,128)(2,1)S(1)}, bf16[160,64,64]{0,2,1:T(8,128)(2,1)}, u32[]{:S(2)}) copy-start(bf16[160,64,64]{0,2,1:T(8,128)(2,1)} %subtract_convert_fusion) | copy-start | bytes 3932164
  403.0 115.2 %all-to-all-start.5 = ((bf16[128,128,64]{1,2,0:T(8,128)(2,1)}), bf16[128,128,64]{1,2,0:T(8,128)(2,1)}, u32[]{:S(2)}, u32[]{:S(2)}) async-start(bf16[128,128,64]{1,2,0:T(8,128)(2,1)} %convolution_convert_fusion), calls=%async_computation.5 | async-start | bytes 4194304 | tf_op jit(solution)/shard_map/all_to_all | solution.py:67
Sparse Core Ops, SparseCore 0:
  175.1 36.1 all-gather.1
  305.5 79.8 all-reduce.1
where the time goes:
time: 529 us; the launch traced here: 528 us
  waiting for transfers between devices  381 us (72%)
  starting transfers between devices  65.5 us (12%)
  local copies, waits for them, and re-layouts  43.1 us (8%)
  matrix products  17.1 us (3%)
  between operations  14.2 us (3%)
  other arithmetic  7.74 us (1%)
    all_to_all x1, waiting for transfers between devices, body(): lax.all_to_all(refreshed, 'own', split_axis=0, concat_axis=0, tiled=True)  95.4 us
    all_to_all x1, waiting for transfers between devices, body(): lax.all_to_all(send_right, 'own', split_axis=0, concat_axis=0, tiled=True)  90.1 us
    psum x1, waiting for transfers between devices, body(): grad_whole = lax.psum(grad_part, 'grp')  75.1 us
    all_to_all x1, waiting for transfers between devices, body(): lax.all_to_all(send_left, 'own', split_axis=0, concat_axis=0, tiled=True)  50.7 us
    all_gather x1, waiting for transfers between devices, body(): old_tables = lax.all_gather(core, 'grp', axis=0, tiled=True)  34.6 us
    all_to_all x1, starting transfers between devices, body(): lax.all_to_all(send_fill, 'own', split_axis=0, concat_axis=0, tiled=True)  18.5 us
    all_to_all x1, starting transfers between devices, body(): lax.all_to_all(refreshed, 'own', split_axis=0, concat_axis=0, tiled=True)  15.8 us
    all_to_all x1, waiting for transfers between devices, body(): lax.all_to_all(send_fill, 'own', split_axis=0, concat_axis=0, tiled=True)  12.7 us
  transfers between devices with their start and end apart: 8, of which 8 were waited for; matrix products, arithmetic and copies ran while one was open for 5% of the time, Pallas kernels for 0%

commit v1 on v0

--- a/solution.py
+++ b/solution.py
@@ -56,7 +56,11 @@
         precision=lax.Precision.HIGHEST,
         preferred_element_type=jnp.float32,
     ).reshape(local_count, rank_width, rank_width)
-    grad_whole = lax.psum(grad_part, "grp")
+    grad_whole = grad_part
+    for hop in (1, 2, 4):
+        grad_whole = grad_whole + lax.ppermute(
+            grad_whole, "grp", [(dev, dev ^ hop) for dev in range(8)]
+        )
     new_tables = (old_tables.astype(jnp.float32) - grad_whole).astype(jnp.bfloat16)
     new_mine = lax.dynamic_slice_in_dim(
         new_tables, lax.axis_index("grp") * per_device, per_device, 0

time: 529 us -> 644 us (1.22)
  waiting for transfers between devices: 381 us -> 485 us
    ppermute x0 -> x3, waiting for transfers between devices: none -> 185 us  [body(): lax.ppermute(grad_whole, 'grp', [(dev, dev ^ hop) for dev in range(8)])]
    psum x1 -> x0, waiting for transfers between devices: 75.1 us -> none  [body(): grad_whole = lax.psum(grad_part, 'grp')]
    ppermute x0 -> x3, starting transfers between devices: none -> 10.9 us  [body(): lax.ppermute(grad_whole, 'grp', [(dev, dev ^ hop) for dev in range(8)])]
    all_to_all x1, starting transfers between devices: 15.8 us -> 5.69 us  [body(): lax.all_to_all(refreshed, 'own', split_axis=0, concat_axis=0, tiled=True)]
  transfers between devices with their start and end apart: 8 -> 10, of which waited for: 8 -> 10; matrix products, arithmetic and copies ran while one was open for 5% -> 4% of each run, Pallas kernels for 0% -> 0%
where the time goes in v1:
time: 644 us; the launch traced here: 637 us
  waiting for transfers between devices  485 us (75%)
  starting transfers between devices  66.2 us (10%)
  local copies, waits for them, and re-layouts  43.2 us (7%)
  matrix products  15.3 us (2%)
  between operations  14.3 us (2%)
  other arithmetic  13.3 us (2%)
    ppermute x3, waiting for transfers between devices, body(): lax.ppermute(grad_whole, 'grp', [(dev, dev ^ hop) for dev in range(8)])  185 us
    all_to_all x1, waiting for transfers between devices, body(): lax.all_to_all(send_right, 'own', split_axis=0, concat_axis=0, tiled=True)  90.1 us
    all_to_all x1, waiting for transfers between devices, body(): lax.all_to_all(refreshed, 'own', split_axis=0, concat_axis=0, tiled=True)  90 us
    all_to_all x1, waiting for transfers between devices, body(): lax.all_to_all(send_left, 'own', split_axis=0, concat_axis=0, tiled=True)  50.7 us
    all_gather x1, waiting for transfers between devices, body(): old_tables = lax.all_gather(core, 'grp', axis=0, tiled=True)  34.6 us
    all_to_all x1, starting transfers between devices, body(): lax.all_to_all(send_fill, 'own', split_axis=0, concat_axis=0, tiled=True)  18.5 us
  transfers between devices with their start and end apart: 10, of which 10 were waited for; matrix products, arithmetic and copies ran while one was open for 4% of the time, Pallas kernels for 0%

profile of v1, /device:TPU:7, one launch (start us, length us, event | category | flops | bytes accessed | tf_op | source)
XLA Modules:
  0.0 636.9 jit_solution(6885791596796367718)
XLA Ops:
  12.0 18.5 %all-to-all-start.1 = ((s32[64,2,1]{1,2,0:T(1,128)}), s32[64,2,1]{1,2,0:T(1,128)S(1)}, u32[]{:S(2)}, u32[]{:S(2)}) async-start(s32[64,2,1]{1,2,0:T(1,128)} %bitcast.4), calls=%async_computation.1 | async-start | bytes 65536 | tf_op jit(solution)/shard_map/all_to_all | solution.py:49
  31.2 12.7 %all-to-all-done.1 = s32[64,2,1]{1,2,0:T(1,128)S(1)} async-done(((s32[64,2,1]{1,2,0:T(1,128)}), s32[64,2,1]{1,2,0:T(1,128)S(1)}, u32[]{:S(2)}, u32[]{:S(2)}) %all-to-all-start.1) | async-done | bytes 544 | tf_op jit(solution)/shard_map/all_to_all | solution.py:49
  43.8 4.6 all-to-all-start
  50.6 11.3 %all-to-all-done = s32[64,2,1]{1,2,0:T(1,128)S(1)} async-done(((s32[64,2,1]{1,2,0:T(1,128)}), s32[64,2,1]{1,2,0:T(1,128)S(1)}, u32[]{:S(2)}, u32[]{:S(2)}) %all-to-all-start) | async-done | bytes 544 | tf_op jit(solution)/shard_map/all_to_all | solution.py:48
  61.9 4.7 all-to-all-start.3
  66.6 3.4 gather_fusion.2
  70.0 90.1 %all-to-all-done.3 = bf16[128,128,64]{1,2,0:T(8,128)(2,1)S(1)} async-done(((bf16[128,128,64]{1,2,0:T(8,128)(2,1)}), bf16[128,128,64]{1,2,0:T(8,128)(2,1)S(1)}, u32[]{:S(2)}, u32[]{:S(2)}) %all-to-all-start.3) | async-done | bytes 2097184 | tf_op jit(solution)/shard_map/all_to_all | solution.py:46
  161.5 10.7 %all-to-all-start.2 = ((bf16[128,128,64]{1,2,0:T(8,128)(2,1)}), bf16[128,128,64]{1,2,0:T(8,128)(2,1)S(1)}, u32[]{:S(2)}, u32[]{:S(2)}) async-start(bf16[128,128,64]{1,2,0:T(8,128)(2,1)} %gather_fusion.2), calls=%async_computation.2 | async-start | bytes 4194304 | tf_op jit(solution)/shard_map/all_to_all | solution.py:45
  176.7 34.6 %all-gather.2.cloned.1.call-done = bf16[160,64,64]{2,1,0:T(8,128)(2,1)} async-done(((bf16[20,64,64]{2,1,0:T(8,128)(2,1)}), bf16[160,64,64]{2,1,0:T(8,128)(2,1)}) %all-gather.2.cloned.1.call-update) | async-done | bytes 1310736 | tf_op jit(solution)/shard_map/all_gather | solution.py:39
  211.3 3.9 gather_fusion.3
  215.2 50.7 %all-to-all-done.2 = bf16[128,128,64]{1,2,0:T(8,128)(2,1)S(1)} async-done(((bf16[128,128,64]{1,2,0:T(8,128)(2,1)}), bf16[128,128,64]{1,2,0:T(8,128)(2,1)S(1)}, u32[]{:S(2)}, u32[]{:S(2)}) %all-to-all-start.2) | async-done | bytes 2097184 | tf_op jit(solution)/shard_map/all_to_all | solution.py:45
  265.9 11.2 %all-to-all-start.4 = ((bf16[64,2,128]{2,1,0:T(2,128)(2,1)}), bf16[64,2,128]{2,1,0:T(2,128)(2,1)S(1)}, u32[]{:S(2)}, u32[]{:S(2)}) async-start(bf16[64,2,128]{2,1,0:T(2,128)(2,1)} %bitcast.6), calls=%async_computation.4 | async-start | bytes 65536 | tf_op jit(solution)/shard_map/all_to_all | solution.py:47
  277.1 3.2 multiply_reduce_fusion
  280.3 10.0 %all-to-all-done.4 = bf16[64,2,128]{2,1,0:T(2,128)(2,1)S(1)} async-done(((bf16[64,2,128]{2,1,0:T(2,128)(2,1)}), bf16[64,2,128]{2,1,0:T(2,128)(2,1)S(1)}, u32[]{:S(2)}, u32[]{:S(2)}) %all-to-all-start.4) | async-done | bytes 32800 | tf_op jit(solution)/shard_map/all_to_all | solution.py:47
  290.4 4.8 fusion
  295.2 4.8 copy.30
  300.0 3.5 fusion.1
  303.5 5.4 collective-permute-start
  308.9 6.8 %collective-permute-done = f32[160,64,64]{0,2,1:T(8,128)S(1)} collective-permute-done((f32[160,64,64]{0,2,1:T(8,128)S(1)}, f32[160,64,64]{0,2,1:T(8,128)S(1)}, u32[]{:S(2)}, u32[]{:S(2)}) %collective-permute-start) | collective-permute-done | bytes 2621472 | tf_op jit(solution)/shard_map/ppermute | solution.py:61
  319.2 91.2 %collective-permute-done.1 = f32[160,64,64]{0,2,1:T(8,128)S(1)} collective-permute-done((f32[160,64,64]{0,2,1:T(8,128)S(1)}, f32[160,64,64]{0,2,1:T(8,128)S(1)}, u32[]{:S(2)}, u32[]{:S(2)}) %collective-permute-start.1) | collective-permute-done | bytes 2621472 | tf_op jit(solution)/shard_map/ppermute | solution.py:61
  410.4 2.8 add.68
  413.2 3.0 collective-permute-start.2
  416.2 4.9 copy.26
  421.2 86.7 %collective-permute-done.2 = f32[160,64,64]{0,2,1:T(8,128)} collective-permute-done((f32[160,64,64]{0,2,1:T(8,128)}, f32[160,64,64]{0,2,1:T(8,128)}, u32[]{:S(2)}, u32[]{:S(2)}) %collective-permute-start.2) | collective-permute-done | bytes 2621472 | tf_op jit(solution)/shard_map/ppermute | solution.py:61
  507.8 6.6 %subtract_convert_fusion = bf16[160,64,64]{0,2,1:T(8,128)(2,1)} fusion(f32[160,64,64]{0,2,1:T(8,128)} %add.68, f32[160,64,64]{0,2,1:T(8,128)} %collective-permute-done.2, bf16[160,64,64]{0,2,1:T(8,128)(2,1)} %copy.26), kind=kLoop, calls=%fused_computation.8 | loop fusion | flops 2621440 | bytes 7864320 | tf_op jit(solution)/shard_map/convert_element_type | solution.py:64
  514.4 5.0 copy.31
  519.4 3.9 gather_fusion.6
  523.3 3.8 convolution_convert_fusion
  527.1 5.7 all-to-all-start.5
  534.3 2.6 copy.33
  536.8 90.0 %all-to-all-done.5 = bf16[128,128,64]{1,2,0:T(8,128)(2,1)} async-done(((bf16[128,128,64]{1,2,0:T(8,128)(2,1)}), bf16[128,128,64]{1,2,0:T(8,128)(2,1)}, u32[]{:S(2)}, u32[]{:S(2)}) %all-to-all-start.5) | async-done | bytes 2097184 | tf_op jit(solution)/shard_map/all_to_all | solution.py:71
  626.8 3.2 gather_fusion.7
  (38 shorter events, 18.5 us)
Async XLA Ops:
  7.2 41.3 %copy-start = (bf16[64,128,64]{1,2,0:T(8,128)(2,1)S(1)}, bf16[64,128,64]{1,2,0:T(8,128)(2,1)}, u32[]{:S(2)}) copy-start(bf16[64,128,64]{1,2,0:T(8,128)(2,1)} %param.7) | copy-start | bytes 3145732
  12.0 31.9 %all-to-all-start.1 = ((s32[64,2,1]{1,2,0:T(1,128)}), s32[64,2,1]{1,2,0:T(1,128)S(1)}, u32[]{:S(2)}, u32[]{:S(2)}) async-start(s32[64,2,1]{1,2,0:T(1,128)} %bitcast.4), calls=%async_computation.1 | async-start | bytes 65536 | tf_op jit(solution)/shard_map/all_to_all | solution.py:49
  43.8 18.1 %all-to-all-start = ((s32[64,2,1]{1,2,0:T(1,128)}), s32[64,2,1]{1,2,0:T(1,128)S(1)}, u32[]{:S(2)}, u32[]{:S(2)}) async-start(s32[64,2,1]{1,2,0:T(1,128)} %bitcast.2), calls=%async_computation | async-start | bytes 65536 | tf_op jit(solution)/shard_map/all_to_all | solution.py:48
  61.9 98.2 %all-to-all-start.3 = ((bf16[128,128,64]{1,2,0:T(8,128)(2,1)}), bf16[128,128,64]{1,2,0:T(8,128)(2,1)S(1)}, u32[]{:S(2)}, u32[]{:S(2)}) async-start(bf16[128,128,64]{1,2,0:T(8,128)(2,1)} %gather_fusion.4), calls=%async_computation.3 | async-start | bytes 4194304 | tf_op jit(solution)/shard_map/all_to_all | solution.py:46
  70.0 102.9 %copy-start.3 = (bf16[64,128]{1,0:T(8,128)(2,1)S(1)}, bf16[64,128]{1,0:T(8,128)(2,1)}, u32[]{:S(2)}) copy-start(bf16[64,128]{1,0:T(8,128)(2,1)} %param.8) | copy-start | bytes 49156
  160.2 1.3 copy-start.1
  161.5 104.4 %all-to-all-start.2 = ((bf16[128,128,64]{1,2,0:T(8,128)(2,1)}), bf16[128,128,64]{1,2,0:T(8,128)(2,1)S(1)}, u32[]{:S(2)}, u32[]{:S(2)}) async-start(bf16[128,128,64]{1,2,0:T(8,128)(2,1)} %gather_fusion.2), calls=%async_computation.2 | async-start | bytes 4194304 | tf_op jit(solution)/shard_map/all_to_all | solution.py:45
  172.2 39.1 %all-gather.2.cloned.1.call-start = ((), (), s32[]{:S(2)}) async-start(), calls=%async_computation.6 | async-start | bytes 2949120 | tf_op jit(solution)/shard_map/all_gather | solution.py:39
  265.9 24.4 %all-to-all-start.4 = ((bf16[64,2,128]{2,1,0:T(2,128)(2,1)}), bf16[64,2,128]{2,1,0:T(2,128)(2,1)S(1)}, u32[]{:S(2)}, u32[]{:S(2)}) async-start(bf16[64,2,128]{2,1,0:T(2,128)(2,1)} %bitcast.6), calls=%async_computation.4 | async-start | bytes 65536 | tf_op jit(solution)/shard_map/all_to_all | solution.py:47
  303.5 12.2 %collective-permute-start = (f32[160,64,64]{0,2,1:T(8,128)S(1)}, f32[160,64,64]{0,2,1:T(8,128)S(1)}, u32[]{:S(2)}, u32[]{:S(2)}) collective-permute-start(f32[160,64,64]{0,2,1:T(8,128)S(1)} %fusion.1), channel_id=1, source_target_pairs={{0,64},{64,0},{128,192},{192,128},{256,320},{320,256},{384,448},{4... | collective-permute-start | bytes 7864328 | tf_op jit(solution)/shard_map/ppermute | solution.py:61
  316.7 93.7 %collective-permute-start.1 = (f32[160,64,64]{0,2,1:T(8,128)S(1)}, f32[160,64,64]{0,2,1:T(8,128)S(1)}, u32[]{:S(2)}, u32[]{:S(2)}) collective-permute-start(f32[160,64,64]{0,2,1:T(8,128)S(1)} %add.67), channel_id=1, source_target_pairs={{0,128},{64,192},{128,0},{192,64},{256,384},{320,448},{384,256},{4... | collective-permute-start | bytes 7864328 | tf_op jit(solution)/shard_map/ppermute | solution.py:61
  413.2 94.6 %collective-permute-start.2 = (f32[160,64,64]{0,2,1:T(8,128)}, f32[160,64,64]{0,2,1:T(8,128)}, u32[]{:S(2)}, u32[]{:S(2)}) collective-permute-start(f32[160,64,64]{0,2,1:T(8,128)} %add.68), channel_id=1, source_target_pairs={{0,256},{64,320},{128,384},{192,448},{256,0},{320,64},{384,128},{4... | collective-permute-start | bytes 7864328 | tf_op jit(solution)/shard_map/ppermute | solution.py:61
  527.1 5.7 copy-start.2
  527.1 99.7 %all-to-all-start.5 = ((bf16[128,128,64]{1,2,0:T(8,128)(2,1)}), bf16[128,128,64]{1,2,0:T(8,128)(2,1)}, u32[]{:S(2)}, u32[]{:S(2)}) async-start(bf16[128,128,64]{1,2,0:T(8,128)(2,1)} %convolution_convert_fusion), calls=%async_computation.5 | async-start | bytes 4194304 | tf_op jit(solution)/shard_map/all_to_all | solution.py:71
Sparse Core Ops, SparseCore 0:
  175.1 36.1 all-gather.1
